TPU v7x, 32 devices: a whole 2x2x4 slice. The times are simulated.
32 devices in a mesh: row: 4 (over z), col: 4 (over y, core), ch: 2 (over x).
Axes of the slice: x: 2, y: 2, z: 4, core: 2. Of those that a mesh axis runs over, the one named last changes fastest.
Arguments:
- spectra: float32 [384, 128, 1024], P('ch', 'row', 'col'), may hold values from 0 to 1
- pixel_factor: float32 [64, 128, 1024], P(None, 'row', 'col'), may hold values from 0.1 to 1
- channel_factor: float32 [64, 384], P(None, 'ch'), may hold values from 0.1 to 1
- labels: int32 [128, 1024], P('row', 'col'), may hold values from 0 to 3
Outputs:
- smoothed_factor: float32 [64, 128, 1024], P(None, 'row', 'col')
- new_channel: float32 [64, 384], P(None, 'ch')
All inputs are finite; a program needn't handle non-finite values.
Results may differ from a plain program's by a relative error of at most 0.000068.
Values sent between devices are 32-bit elements; how exact they have to be, the bound alone decides.
A program may use at most 64 MiB of HBM per device.

v0:
```python
import jax
import jax.numpy as jnp
from jax import lax
from jax.sharding import PartitionSpec as P

SMOOTH = 3
epsilon = 1e-09


def padded_2(block, sides, width):
    for axis, dim in sides:
        count = lax.axis_size(axis)
        forward = [(i, i + 1) for i in range(count - 1)]
        backward = [(target, source) for source, target in forward]
        low = lax.ppermute(
            lax.slice_in_dim(block, block.shape[dim] - width, None, axis=dim), axis, forward
        )
        high = lax.ppermute(lax.slice_in_dim(block, 0, width, axis=dim), axis, backward)
        block = jnp.concatenate([low, block, high], axis=dim)
    return block


def coefficients(marked):
    center = marked[1:-1, 1:-1]
    result = []
    for neighbour in (marked[:-2, 1:-1], marked[2:, 1:-1], marked[1:-1, :-2], marked[1:-1, 2:]):
        result.append(
            jnp.where(neighbour == 0, 0.0, jnp.where(neighbour == center, 1.0, 0.25)).astype(
                jnp.float32
            )
        )
    return result


def smooth_once(padded, field, weights):
    combined = field + weights[0] * padded[:, :-2, 1:-1] + weights[1] * padded[:, 2:, 1:-1]
    combined = combined + weights[2] * padded[:, 1:-1, :-2] + weights[3] * padded[:, 1:-1, 2:]
    return combined / (1.0 + weights[0] + weights[1] + weights[2] + weights[3])


def lift_factor(own_factor, pixel_top, chan_gram):
    factor_rank = own_factor.shape[0]
    flat_own = own_factor.reshape(factor_rank, -1)
    lower = jnp.dot(
        chan_gram, flat_own, precision=lax.Precision.HIGHEST, preferred_element_type=jnp.float32
    )
    return (flat_own * pixel_top.reshape(factor_rank, -1) / (lower + epsilon)).reshape(
        own_factor.shape
    )


def shards(spectra, pixel_factor, channel_factor, labels):
    precise = lax.Precision.HIGHEST
    contraction = (((1,), (1,)), ((), ()))
    factor_rank, row_count, col_count = pixel_factor.shape
    flat_pixel = pixel_factor.reshape(factor_rank, row_count * col_count)
    flat_data = spectra.reshape(spectra.shape[0], row_count * col_count)
    chan_top = lax.dot_general(
        flat_pixel, flat_data, contraction, precision=precise, preferred_element_type=jnp.float32
    )
    pixel_gram = lax.dot_general(
        flat_pixel, flat_pixel, contraction, precision=precise, preferred_element_type=jnp.float32
    )
    chan_top, pixel_gram = lax.psum((chan_top, pixel_gram), ("row", "col"))
    new_channel = (
        channel_factor
        * chan_top
        / (
            jnp.dot(
                pixel_gram, channel_factor, precision=precise, preferred_element_type=jnp.float32
            )
            + epsilon
        )
    )
    part_top = jnp.dot(
        new_channel, flat_data, precision=precise, preferred_element_type=jnp.float32
    ).reshape(factor_rank, row_count, col_count)
    part_gram = lax.dot_general(
        new_channel, new_channel, contraction, precision=precise, preferred_element_type=jnp.float32
    )
    marked = labels + 1
    share_rows = row_count // lax.axis_size("ch")
    share_start = lax.axis_index("ch") * share_rows
    pixel_top = lax.psum_scatter(part_top, "ch", scatter_dimension=1, tiled=True)
    chan_gram = lax.psum(part_gram, "ch")
    own_factor = lax.dynamic_slice_in_dim(pixel_factor, share_start, share_rows, 1)
    own_marks = lax.dynamic_slice_in_dim(marked, share_start, share_rows, 0)
    field = lift_factor(own_factor, pixel_top, chan_gram)
    border_marks = padded_2(own_marks, ((("row", "ch"), 0), ("col", 1)), 1)
    weights = coefficients(border_marks)
    for iteration in range(SMOOTH):
        padded = padded_2(field, ((("row", "ch"), 1), ("col", 2)), 1)
        field = smooth_once(padded, field, weights)
    smoothed_factor = lax.all_gather(field, "ch", axis=1, tiled=True)
    return (smoothed_factor, new_channel)


def solution(mesh):
    placed = (P("ch", "row", "col"), P(None, "row", "col"), P(None, "ch"), P("row", "col"))
    return jax.shard_map(
        shards,
        mesh=mesh,
        in_specs=placed,
        out_specs=(P(None, "row", "col"), P(None, "ch")),
        check_vma=False,
    )
```

profile of v0, /device:TPU:0, one launch (start us, length us, event | category | flops | bytes accessed | tf_op | source)
XLA Modules:
  0.0 290.6 jit_solution(9528814193666715446)
XLA Ops:
  7.2 7.0 %fusion.42 = f32[64,64]{1,0:T(8,128)} fusion(f32[64,32,256]{2,1,0:T(8,128)} %param.5), kind=kOutput, calls=%fused_computation.64 | convolution fusion | flops 402653184 | bytes 2113536 | tf_op jit(solution)/shard_map/dot_general | solution.py:61
  14.2 12.2 %fusion.36 = f32[64,192]{1,0:T(8,128)} fusion(f32[192,32,256]{2,1,0:T(8,128)} %param.4, f32[64,32,256]{2,1,0:T(8,128)S(1)} %copy-done.2), kind=kOutput, calls=%fused_computation.61 | convolution fusion | flops 1207959552 | bytes 8437760 | tf_op jit(solution)/shard_map/dot_general | solution.py:58
  26.5 0.2 reduce-scatter.2.cloned.1.call-start
  26.7 91.5 %all-reduce.3.cloned.1.call-done = (f32[64,64]{1,0:T(8,128)}, f32[64,192]{1,0:T(8,128)}) async-done(((f32[64,64]{1,0:T(8,128)}, f32[64,192]{1,0:T(8,128)}), (f32[64,64]{1,0:T(8,128)}, f32[64,192]{1,0:T(8,128)})) %all-reduce.3.cloned.1.call-update) | async-done | bytes 65552 | tf_op jit(solution)/shard_map/psum | solution.py:64
  118.2 1.1 fusion.41
  119.3 11.4 %fusion = f32[64,32,256]{2,0,1:T(8,128)} fusion(f32[64,192]{1,0:T(8,128)S(1)} %fusion.41, f32[24,8,32,256]{3,2,1,0:T(8,128)} %bitcast.30), kind=kOutput, calls=%fused_computation | convolution fusion | flops 1207959552 | bytes 8437760 | tf_op jit(solution)/shard_map/dot_general | solution.py:75
  130.8 0.7 copy-done.4
  131.5 1.3 collective-permute-start.2
  132.8 4.5 %collective-permute-start = (s32[1,256]{1,0:T(1,128)S(1)}, s32[1,256]{1,0:T(1,128)S(1)}, u32[]{:S(2)}, u32[]{:S(2)}) collective-permute-start(s32[1,256]{1,0:T(1,128)S(1)} %get-tuple-element.34), channel_id=1, source_target_pairs={{0,1},{1,8},{8,9},{9,16},{16,17},{17,24},{24,25},{2,3},{3,10},{10,... | collective-permute-start | bytes 3080 | tf_op jit(solution)/shard_map/ppermute | solution.py:15
  137.4 0.6 copy.164
  138.0 0.6 collective-permute-done
  138.6 0.2 fusion.55
  138.8 10.2 %psum.23 = f32[64,64]{1,0:T(8,128)S(1)} all-reduce(f32[64,64]{1,0:T(8,128)S(1)} %fusion.55), channel_id=1, replica_groups=mesh['row'=4,'col'=4,'ch'=2] {'ch'}, use_global_device_ids=true, to_apply=%region_3.0 | all-reduce | flops 4096 | bytes 32768 | tf_op jit(solution)/shard_map/psum | solution.py:85
  149.0 13.5 %reduce-scatter.2.cloned.1.call-done = f32[64,16,256]{2,0,1:T(8,128)} async-done(((f32[64,32,256]{2,0,1:T(8,128)}), f32[64,16,256]{2,0,1:T(8,128)}) %reduce-scatter.2.cloned.1.call-update) | async-done | bytes 1048592 | tf_op jit(solution)/shard_map/reduce_scatter | solution.py:84
  162.5 1.3 copy.163
  163.8 1.1 fusion.5
  165.0 0.3 copy.166
  165.4 1.3 collective-permute-start.3
  166.7 4.5 %collective-permute-start.1 = (f32[64,1,256]{2,0,1:T(8,128)S(1)}, f32[64,1,256]{2,0,1:T(8,128)S(1)}, u32[]{:S(2)}, u32[]{:S(2)}) collective-permute-start(f32[64,1,256]{2,0,1:T(8,128)S(1)} %copy.160), channel_id=1, source_target_pairs={{0,1},{1,8},{8,9},{9,16},{16,17},{17,24},{24,25},{2,3},{3,10},{10,... | collective-permute-start | bytes 196616 | tf_op jit(solution)/shard_map/ppermute | solution.py:15
  171.4 1.3 collective-permute-start.6
  172.7 3.0 %collective-permute-start.4 = (s32[18,1]{1,0:T(8,128)S(1)}, s32[18,1]{1,0:T(8,128)S(1)}, u32[]{:S(2)}, u32[]{:S(2)}) collective-permute-start(s32[18,1]{1,0:T(8,128)S(1)} %get-tuple-element.32), channel_id=1, source_target_pairs={{0,2},{2,4},{4,6},{1,3},{3,5},{5,7},{8,10},{10,12},{12,14},{9,11},... | collective-permute-start | bytes 224 | tf_op jit(solution)/shard_map/ppermute | solution.py:15
  175.7 1.6 copy.135
  177.5 3.0 %collective-permute-start.5 = (f32[64,18,1]{0,1,2:T(8,128)S(1)}, f32[64,18,1]{0,1,2:T(8,128)S(1)}, u32[]{:S(2)}, u32[]{:S(2)}) collective-permute-start(f32[64,18,1]{0,1,2:T(8,128)S(1)} %get-tuple-element.23), channel_id=1, source_target_pairs={{0,2},{2,4},{4,6},{1,3},{3,5},{5,7},{8,10},{10,12},{12,14},{9,11},... | collective-permute-start | bytes 13832 | tf_op jit(solution)/shard_map/ppermute | solution.py:15
  180.5 1.5 collective-permute-start.7
  182.2 0.1 copy.145
  182.7 0.9 collective-permute-done.7
  183.6 9.2 %fusion.26 = f32[64,16,256]{0,1,2:T(8,128)S(1)} fusion(f32[64,18,1]{0,1,2:T(8,128)S(1)} %collective-permute-done.7, f32[64,1,256]{0,1,2:T(1,128)S(1)} %copy.139, f32[64,16,256]{0,1,2:T(8,128)} %copy-done.1, f32[64,1,256]{0,1,2:T(1,128)S(1)} %copy.133, f32[64,18,1]{0,1,2:T(8,128)S(1)} %collective-permute-done.5, f32[16,256]{0,1:T(8,128)S(1)} %copy.145, ...), kind=kLoop, calls=%fused_computation.44 | loop fusion | flops 4456448 | bytes 2319360 | tf_op jit(solution)/shard_map/div | solution.py:38
  192.8 0.2 fusion.51
  193.1 1.3 collective-permute-start.9
  194.5 4.5 %collective-permute-start.8 = (f32[64,1,256]{2,0,1:T(8,128)S(1)}, f32[64,1,256]{2,0,1:T(8,128)S(1)}, u32[]{:S(2)}, u32[]{:S(2)}) collective-permute-start(f32[64,1,256]{2,0,1:T(8,128)S(1)} %copy.146), channel_id=1, source_target_pairs={{0,1},{1,8},{8,9},{9,16},{16,17},{17,24},{24,25},{2,3},{3,10},{10,... | collective-permute-start | bytes 196616 | tf_op jit(solution)/shard_map/ppermute | solution.py:15
  199.0 0.2 collective-permute-done.9
  199.4 2.0 collective-permute-done.8
  201.4 2.8 collective-permute-start.10
  204.3 1.3 collective-permute-start.11
  205.6 2.4 collective-permute-done.11
  208.0 9.2 %fusion.17 = f32[64,16,256]{0,1,2:T(8,128)S(1)} fusion(f32[64,18,1]{0,1,2:T(8,128)S(1)} %collective-permute-done.11, f32[64,1,256]{0,1,2:T(1,128)S(1)} %copy.149, f32[64,16,256]{0,1,2:T(8,128)} %copy-done, f32[64,1,256]{0,1,2:T(1,128)S(1)} %copy.147, f32[64,18,1]{0,1,2:T(8,128)S(1)} %collective-permute-done.10, f32[16,256]{0,1:T(8,128)S(1)} %copy.145, ...), kind=kLoop, calls=%fused_computation.27 | loop fusion | flops 4456448 | bytes 2319360 | tf_op jit(solution)/shard_map/div | solution.py:38
  217.2 0.2 fusion.50
  217.5 1.3 collective-permute-start.13
  218.9 4.9 %collective-permute-start.12 = (f32[64,1,256]{2,0,1:T(8,128)S(1)}, f32[64,1,256]{2,0,1:T(8,128)S(1)}, u32[]{:S(2)}, u32[]{:S(2)}) collective-permute-start(f32[64,1,256]{2,0,1:T(8,128)S(1)} %copy.152), channel_id=1, source_target_pairs={{0,1},{1,8},{8,9},{9,16},{16,17},{17,24},{24,25},{2,3},{3,10},{10,... | collective-permute-start | bytes 196616 | tf_op jit(solution)/shard_map/ppermute | solution.py:15
  223.8 0.2 collective-permute-done.13
  224.1 1.6 collective-permute-done.12
  225.8 3.6 %collective-permute-start.14 = (f32[64,18,1]{0,1,2:T(8,128)S(1)}, f32[64,18,1]{0,1,2:T(8,128)S(1)}, u32[]{:S(2)}, u32[]{:S(2)}) collective-permute-start(f32[64,18,1]{0,1,2:T(8,128)S(1)} %get-tuple-element.19), channel_id=1, source_target_pairs={{0,2},{2,4},{4,6},{1,3},{3,5},{5,7},{8,10},{10,12},{12,14},{9,11},... | collective-permute-start | bytes 13832 | tf_op jit(solution)/shard_map/ppermute | solution.py:15
  229.4 1.3 collective-permute-start.15
  230.7 2.1 collective-permute-done.15
  232.7 5.2 %fusion.8 = f32[64,16,256]{0,1,2:T(8,128)} fusion(f32[64,18,1]{0,1,2:T(8,128)S(1)} %collective-permute-done.15, f32[64,1,256]{0,1,2:T(1,128)S(1)} %copy.155, f32[64,16,256]{0,1,2:T(8,128)S(1)} %fusion.17, f32[64,1,256]{0,1,2:T(1,128)S(1)} %copy.153, f32[64,18,1]{0,1,2:T(8,128)S(1)} %collective-permute-done.14, f32[16,256]{0,1:T(8,128)S(1)} %copy.145, ...), kind=kLoop, calls=%fused_computation.10 | loop fusion | flops 4456448 | bytes 2319360 | tf_op jit(solution)/shard_map/div | solution.py:38
  237.9 3.5 %copy.158 = f32[64,16,256]{2,0,1:T(8,128)} copy(f32[64,16,256]{0,1,2:T(8,128)} %fusion.8) | data formatting | bytes 2097152 | tf_op jit(solution)/shard_map/div | solution.py:38
  241.4 38.5 %all-gather.2.cloned.1.call-done = f32[64,32,256]{2,0,1:T(8,128)} async-done(((f32[64,16,256]{2,0,1:T(8,128)}), f32[64,32,256]{2,0,1:T(8,128)}) %all-gather.2.cloned.1.call-update) | async-done | bytes 2097168 | tf_op jit(solution)/shard_map/all_gather | solution.py:94
  280.0 4.1 %copy.159 = f32[64,32,256]{2,1,0:T(8,128)} copy(f32[64,32,256]{2,0,1:T(8,128)} %all-gather.2.cloned.1.call-done) | data formatting | bytes 4194304
  (50 shorter events, 1.9 us)
Async XLA Ops:
  7.2 7.1 %copy-start.2 = (f32[64,32,256]{2,1,0:T(8,128)S(1)}, f32[64,32,256]{2,1,0:T(8,128)}, u32[]{:S(2)}) copy-start(f32[64,32,256]{2,1,0:T(8,128)} %param.5) | copy-start | bytes 6291460
  7.2 111.1 %all-reduce.3.cloned.1.call-start = ((), (), s32[]{:S(2)}) async-start(), calls=%async_computation.3 | async-start | bytes 196608 | tf_op jit(solution)/shard_map/psum | solution.py:64
  14.2 104.0 %copy-start.5 = (f32[64,192]{1,0:T(8,128)S(1)}, f32[64,192]{1,0:T(8,128)}, u32[]{:S(2)}) copy-start(f32[64,192]{1,0:T(8,128)} %param.6) | copy-start | bytes 147460
  26.5 136.1 %reduce-scatter.2.cloned.1.call-start = ((), (), s32[]{:S(2)}) async-start(), calls=%async_computation.1 | async-start | bytes 3145728 | tf_op jit(solution)/shard_map/reduce_scatter | solution.py:84
  119.3 19.3 %copy-start.3 = (f32[64,192]{1,0:T(8,128)}, f32[64,192]{1,0:T(8,128)S(1)}, u32[]{:S(2)}) copy-start(f32[64,192]{1,0:T(8,128)S(1)} %fusion.41) | copy-start | bytes 147460
  130.7 0.8 copy-start.4
  130.7 149.3 %all-gather.2.cloned.1.call-start = ((), (), s32[]{:S(2)}) async-start(), calls=%async_computation.2 | async-start | bytes 3145728 | tf_op jit(solution)/shard_map/all_gather | solution.py:94
  131.5 6.6 %collective-permute-start.2 = (s32[1,256]{1,0:T(1,128)S(1)}, s32[1,256]{1,0:T(1,128)S(1)}, u32[]{:S(2)}, u32[]{:S(2)}) collective-permute-start(s32[1,256]{1,0:T(1,128)S(1)} %get-tuple-element.33), channel_id=1, source_target_pairs={{1,0},{8,1},{9,8},{16,9},{17,16},{24,17},{25,24},{3,2},{10,3},{11,... | collective-permute-start | bytes 3080 | tf_op jit(solution)/shard_map/ppermute | solution.py:18
  132.8 5.8 %collective-permute-start = (s32[1,256]{1,0:T(1,128)S(1)}, s32[1,256]{1,0:T(1,128)S(1)}, u32[]{:S(2)}, u32[]{:S(2)}) collective-permute-start(s32[1,256]{1,0:T(1,128)S(1)} %get-tuple-element.34), channel_id=1, source_target_pairs={{0,1},{1,8},{8,9},{9,16},{16,17},{17,24},{24,25},{2,3},{3,10},{10,... | collective-permute-start | bytes 3080 | tf_op jit(solution)/shard_map/ppermute | solution.py:15
  165.4 11.9 %collective-permute-start.3 = (f32[64,1,256]{2,0,1:T(8,128)S(1)}, f32[64,1,256]{2,0,1:T(8,128)S(1)}, u32[]{:S(2)}, u32[]{:S(2)}) collective-permute-start(f32[64,1,256]{2,0,1:T(8,128)S(1)} %copy.161), channel_id=1, source_target_pairs={{1,0},{8,1},{9,8},{16,9},{17,16},{24,17},{25,24},{3,2},{10,3},{11,... | collective-permute-start | bytes 196616 | tf_op jit(solution)/shard_map/ppermute | solution.py:18
  166.7 10.7 %collective-permute-start.1 = (f32[64,1,256]{2,0,1:T(8,128)S(1)}, f32[64,1,256]{2,0,1:T(8,128)S(1)}, u32[]{:S(2)}, u32[]{:S(2)}) collective-permute-start(f32[64,1,256]{2,0,1:T(8,128)S(1)} %copy.160), channel_id=1, source_target_pairs={{0,1},{1,8},{8,9},{9,16},{16,17},{17,24},{24,25},{2,3},{3,10},{10,... | collective-permute-start | bytes 196616 | tf_op jit(solution)/shard_map/ppermute | solution.py:15
  171.4 10.7 %collective-permute-start.6 = (s32[18,1]{1,0:T(8,128)S(1)}, s32[18,1]{1,0:T(8,128)S(1)}, u32[]{:S(2)}, u32[]{:S(2)}) collective-permute-start(s32[18,1]{1,0:T(8,128)S(1)} %get-tuple-element.31), channel_id=1, source_target_pairs={{2,0},{4,2},{6,4},{3,1},{5,3},{7,5},{10,8},{12,10},{14,12},{11,9},... | collective-permute-start | bytes 224 | tf_op jit(solution)/shard_map/ppermute | solution.py:18
  172.7 9.4 %collective-permute-start.4 = (s32[18,1]{1,0:T(8,128)S(1)}, s32[18,1]{1,0:T(8,128)S(1)}, u32[]{:S(2)}, u32[]{:S(2)}) collective-permute-start(s32[18,1]{1,0:T(8,128)S(1)} %get-tuple-element.32), channel_id=1, source_target_pairs={{0,2},{2,4},{4,6},{1,3},{3,5},{5,7},{8,10},{10,12},{12,14},{9,11},... | collective-permute-start | bytes 224 | tf_op jit(solution)/shard_map/ppermute | solution.py:15
  177.3 5.4 %copy-start.1 = (f32[64,16,256]{0,1,2:T(8,128)}, f32[64,16,256]{0,1,2:T(8,128)S(1)}, u32[]{:S(2)}) copy-start(f32[64,16,256]{0,1,2:T(8,128)S(1)} %copy.135) | copy-start | bytes 3145732
  177.5 5.1 %collective-permute-start.5 = (f32[64,18,1]{0,1,2:T(8,128)S(1)}, f32[64,18,1]{0,1,2:T(8,128)S(1)}, u32[]{:S(2)}, u32[]{:S(2)}) collective-permute-start(f32[64,18,1]{0,1,2:T(8,128)S(1)} %get-tuple-element.23), channel_id=1, source_target_pairs={{0,2},{2,4},{4,6},{1,3},{3,5},{5,7},{8,10},{10,12},{12,14},{9,11},... | collective-permute-start | bytes 13832 | tf_op jit(solution)/shard_map/ppermute | solution.py:15
  180.5 3.1 %collective-permute-start.7 = (f32[64,18,1]{0,1,2:T(8,128)S(1)}, f32[64,18,1]{0,1,2:T(8,128)S(1)}, u32[]{:S(2)}, u32[]{:S(2)}) collective-permute-start(f32[64,18,1]{0,1,2:T(8,128)S(1)} %get-tuple-element.24), channel_id=1, source_target_pairs={{2,0},{4,2},{6,4},{3,1},{5,3},{7,5},{10,8},{12,10},{14,12},{11,9},... | collective-permute-start | bytes 13832 | tf_op jit(solution)/shard_map/ppermute | solution.py:18
  192.8 12.8 %copy-start = (f32[64,16,256]{0,1,2:T(8,128)}, f32[64,16,256]{0,1,2:T(8,128)S(1)}, u32[]{:S(2)}) copy-start(f32[64,16,256]{0,1,2:T(8,128)S(1)} %fusion.26) | copy-start | bytes 3145732
  193.1 6.2 %collective-permute-start.9 = (f32[64,1,256]{2,0,1:T(8,128)S(1)}, f32[64,1,256]{2,0,1:T(8,128)S(1)}, u32[]{:S(2)}, u32[]{:S(2)}) collective-permute-start(f32[64,1,256]{2,0,1:T(8,128)S(1)} %copy.148), channel_id=1, source_target_pairs={{1,0},{8,1},{9,8},{16,9},{17,16},{24,17},{25,24},{3,2},{10,3},{11,... | collective-permute-start | bytes 196616 | tf_op jit(solution)/shard_map/ppermute | solution.py:18
  194.5 6.8 %collective-permute-start.8 = (f32[64,1,256]{2,0,1:T(8,128)S(1)}, f32[64,1,256]{2,0,1:T(8,128)S(1)}, u32[]{:S(2)}, u32[]{:S(2)}) collective-permute-start(f32[64,1,256]{2,0,1:T(8,128)S(1)} %copy.146), channel_id=1, source_target_pairs={{0,1},{1,8},{8,9},{9,16},{16,17},{17,24},{24,25},{2,3},{3,10},{10,... | collective-permute-start | bytes 196616 | tf_op jit(solution)/shard_map/ppermute | solution.py:15
  201.4 4.1 %collective-permute-start.10 = (f32[64,18,1]{0,1,2:T(8,128)S(1)}, f32[64,18,1]{0,1,2:T(8,128)S(1)}, u32[]{:S(2)}, u32[]{:S(2)}) collective-permute-start(f32[64,18,1]{0,1,2:T(8,128)S(1)} %get-tuple-element.21), channel_id=1, source_target_pairs={{0,2},{2,4},{4,6},{1,3},{3,5},{5,7},{8,10},{10,12},{12,14},{9,11},... | collective-permute-start | bytes 13832 | tf_op jit(solution)/shard_map/ppermute | solution.py:15
  204.3 3.7 %collective-permute-start.11 = (f32[64,18,1]{0,1,2:T(8,128)S(1)}, f32[64,18,1]{0,1,2:T(8,128)S(1)}, u32[]{:S(2)}, u32[]{:S(2)}) collective-permute-start(f32[64,18,1]{0,1,2:T(8,128)S(1)} %get-tuple-element.22), channel_id=1, source_target_pairs={{2,0},{4,2},{6,4},{3,1},{5,3},{7,5},{10,8},{12,10},{14,12},{11,9},... | collective-permute-start | bytes 13832 | tf_op jit(solution)/shard_map/ppermute | solution.py:18
  217.5 6.5 %collective-permute-start.13 = (f32[64,1,256]{2,0,1:T(8,128)S(1)}, f32[64,1,256]{2,0,1:T(8,128)S(1)}, u32[]{:S(2)}, u32[]{:S(2)}) collective-permute-start(f32[64,1,256]{2,0,1:T(8,128)S(1)} %copy.154), channel_id=1, source_target_pairs={{1,0},{8,1},{9,8},{16,9},{17,16},{24,17},{25,24},{3,2},{10,3},{11,... | collective-permute-start | bytes 196616 | tf_op jit(solution)/shard_map/ppermute | solution.py:18
  218.9 6.8 %collective-permute-start.12 = (f32[64,1,256]{2,0,1:T(8,128)S(1)}, f32[64,1,256]{2,0,1:T(8,128)S(1)}, u32[]{:S(2)}, u32[]{:S(2)}) collective-permute-start(f32[64,1,256]{2,0,1:T(8,128)S(1)} %copy.152), channel_id=1, source_target_pairs={{0,1},{1,8},{8,9},{9,16},{16,17},{17,24},{24,25},{2,3},{3,10},{10,... | collective-permute-start | bytes 196616 | tf_op jit(solution)/shard_map/ppermute | solution.py:15
  225.8 4.9 %collective-permute-start.14 = (f32[64,18,1]{0,1,2:T(8,128)S(1)}, f32[64,18,1]{0,1,2:T(8,128)S(1)}, u32[]{:S(2)}, u32[]{:S(2)}) collective-permute-start(f32[64,18,1]{0,1,2:T(8,128)S(1)} %get-tuple-element.19), channel_id=1, source_target_pairs={{0,2},{2,4},{4,6},{1,3},{3,5},{5,7},{8,10},{10,12},{12,14},{9,11},... | collective-permute-start | bytes 13832 | tf_op jit(solution)/shard_map/ppermute | solution.py:15
  229.4 3.4 %collective-permute-start.15 = (f32[64,18,1]{0,1,2:T(8,128)S(1)}, f32[64,18,1]{0,1,2:T(8,128)S(1)}, u32[]{:S(2)}, u32[]{:S(2)}) collective-permute-start(f32[64,18,1]{0,1,2:T(8,128)S(1)} %get-tuple-element.20), channel_id=1, source_target_pairs={{2,0},{4,2},{6,4},{3,1},{5,3},{7,5},{10,8},{12,10},{14,12},{11,9},... | collective-permute-start | bytes 13832 | tf_op jit(solution)/shard_map/ppermute | solution.py:18
Sparse Core Ops, SparseCore 0:
  26.6 91.6 all-reduce.2
  130.8 31.6 reduce-scatter.1
  241.6 38.3 all-gather.1
where the time goes:
time: 292 us; the launch traced here: 291 us
  waiting for transfers between devices  154 us (53%)
  starting transfers between devices  41.8 us (14%)
  matrix products  33 us (11%)
  other arithmetic  23.7 us (8%)
  between operations  14.2 us (5%)
  local copies, waits for them, and re-layouts  14.1 us (5%)
  blocking collectives  10.2 us (3%)
    psum x1, waiting for transfers between devices, shards(): chan_top, pixel_gram = lax.psum((chan_top, pixel_gram), ('row', 'col'))  91.5 us
    all_gather x1, waiting for transfers between devices, shards(): smoothed_factor = lax.all_gather(field, 'ch', axis=1, tiled=True)  38.5 us
    ppermute x8, starting transfers between devices, padded_2(): lax.ppermute(lax.slice_in_dim(block, block.shape[dim] - width, None, axis...  31 us
    div x3, other arithmetic, smooth_once(): return combined / (1.0 + weights[0] + weights[1] + weights[2] + weights[3])  23.6 us
    reduce_scatter x1, waiting for transfers between devices, shards(): lax.psum_scatter(part_top, 'ch', scatter_dimension=1, tiled=True)  13.5 us
    dot_general x1, matrix products, shards(): lax.dot_general(flat_pixel, flat_data, contraction, precision=precise, pr...  12.2 us
    dot_general x1, matrix products, shards(): jnp.dot(new_channel, flat_data, precision=precise, preferred_element_type...  11.4 us
    ppermute x8, starting transfers between devices, padded_2(): lax.ppermute(lax.slice_in_dim(block, 0, width, axis=dim), axis, backward)  10.5 us
  transfers between devices with their start and end apart: 19, of which 11 were waited for; matrix products, arithmetic and copies ran while one was open for 1% of the time, Pallas kernels for 0%

commit v1 on v0

--- a/solution.py
+++ b/solution.py
@@ -91,7 +91,10 @@
     for iteration in range(SMOOTH):
         padded = padded_2(field, ((("row", "ch"), 1), ("col", 2)), 1)
         field = smooth_once(padded, field, weights)
-    smoothed_factor = lax.all_gather(field, "ch", axis=1, tiled=True)
+    size = lax.axis_size("ch")
+    blocks = jnp.stack([field for _ in range(size)])
+    blocks = lax.all_to_all(blocks, "ch", split_axis=0, concat_axis=0)
+    smoothed_factor = jnp.concatenate(blocks, axis=1)
     return (smoothed_factor, new_channel)
 
 

time: 292 us -> 276 us (0.945)
  blocking collectives: 10.2 us -> 37.6 us
  waiting for transfers between devices: 154 us -> 127 us
  other arithmetic: 23.7 us -> 17.1 us
  local copies, waits for them, and re-layouts: 14.1 us -> 8.37 us
  starting transfers between devices: 41.8 us -> 36.6 us
    all_gather x1 -> x0, waiting for transfers between devices: 38.5 us -> none  [shards(): smoothed_factor = lax.all_gather(field, 'ch', axis=1, tiled=True)]
    all_to_all x0 -> x1, blocking collectives: none -> 27.3 us  [shards(): blocks = lax.all_to_all(blocks, 'ch', split_axis=0, concat_axis=0)]
    div x3 -> x2, other arithmetic: 23.6 us -> 9.66 us  [smooth_once(): return combined / (1.0 + weights[0] + weights[1] + weights[2] + weights[3])]
    ppermute x8, waiting for transfers between devices: 5.83 us -> 19.3 us  [padded_2(): lax.ppermute(lax.slice_in_dim(block, 0, width, axis=dim), axis, backward)]
    another operation x0 -> x2, other arithmetic: none -> 7.25 us  [shards(): blocks = jnp.stack([field for _ in range(size)])]
    ppermute x8, starting transfers between devices: 31 us -> 26 us  [padded_2(): lax.ppermute(lax.slice_in_dim(block, block.shape[dim] - width, None, axis...]
    unnamed x17 -> x9, local copies, waits for them, and re-layouts: 5.77 us -> 1.35 us
    div x1 -> x0, local copies, waits for them, and re-layouts: 3.47 us -> none  [smooth_once(): return combined / (1.0 + weights[0] + weights[1] + weights[2] + weights[3])]
  transfers between devices with their start and end apart: 19 -> 18, of which waited for: 11 -> 11; matrix products, arithmetic and copies ran while one was open for 1% -> 0% of each run, Pallas kernels for 0% -> 0%
where the time goes in v1:
time: 276 us; the launch traced here: 274 us
  waiting for transfers between devices  127 us (46%)
  blocking collectives  37.6 us (14%)
  starting transfers between devices  36.6 us (13%)
  matrix products  33 us (12%)
  other arithmetic  17.1 us (6%)
  between operations  14.4 us (5%)
  local copies, waits for them, and re-layouts  8.37 us (3%)
    psum x1, waiting for transfers between devices, shards(): chan_top, pixel_gram = lax.psum((chan_top, pixel_gram), ('row', 'col'))  91.5 us
    all_to_all x1, blocking collectives, shards(): blocks = lax.all_to_all(blocks, 'ch', split_axis=0, concat_axis=0)  27.3 us
    ppermute x8, starting transfers between devices, padded_2(): lax.ppermute(lax.slice_in_dim(block, block.shape[dim] - width, None, axis...  26 us
    ppermute x8, waiting for transfers between devices, padded_2(): lax.ppermute(lax.slice_in_dim(block, 0, width, axis=dim), axis, backward)  19.3 us
    reduce_scatter x1, waiting for transfers between devices, shards(): lax.psum_scatter(part_top, 'ch', scatter_dimension=1, tiled=True)  13.5 us
    dot_general x1, matrix products, shards(): lax.dot_general(flat_pixel, flat_data, contraction, precision=precise, pr...  12.2 us
    dot_general x1, matrix products, shards(): jnp.dot(new_channel, flat_data, precision=precise, preferred_element_type...  11.4 us
    ppermute x8, starting transfers between devices, padded_2(): lax.ppermute(lax.slice_in_dim(block, 0, width, axis=dim), axis, backward)  10.3 us
  transfers between devices with their start and end apart: 18, of which 11 were waited for; matrix products, arithmetic and copies ran while one was open for 0% of the time, Pallas kernels for 0%

profile of v1, /device:TPU:0, one launch (start us, length us, event | category | flops | bytes accessed | tf_op | source)
XLA Modules:
  0.0 274.3 jit_solution(5186106116190904063)
XLA Ops:
  7.2 7.0 %fusion.43 = f32[64,64]{1,0:T(8,128)} fusion(f32[64,32,256]{2,1,0:T(8,128)} %param.5), kind=kOutput, calls=%fused_computation.66 | convolution fusion | flops 402653184 | bytes 2113536 | tf_op jit(solution)/shard_map/dot_general | solution.py:61
  14.2 12.2 %fusion.37 = f32[64,192]{1,0:T(8,128)} fusion(f32[192,32,256]{2,1,0:T(8,128)} %param.4, f32[64,32,256]{2,1,0:T(8,128)S(1)} %copy-done), kind=kOutput, calls=%fused_computation.63 | convolution fusion | flops 1207959552 | bytes 8437760 | tf_op jit(solution)/shard_map/dot_general | solution.py:58
  26.5 0.2 reduce-scatter.2.cloned.1.call-start
  26.7 91.5 %all-reduce.3.cloned.1.call-done = (f32[64,64]{1,0:T(8,128)}, f32[64,192]{1,0:T(8,128)}) async-done(((f32[64,64]{1,0:T(8,128)}, f32[64,192]{1,0:T(8,128)}), (f32[64,64]{1,0:T(8,128)}, f32[64,192]{1,0:T(8,128)})) %all-reduce.3.cloned.1.call-update) | async-done | bytes 65552 | tf_op jit(solution)/shard_map/psum | solution.py:64
  118.2 1.1 fusion.42
  119.3 11.4 %fusion = f32[64,32,256]{2,0,1:T(8,128)} fusion(f32[64,192]{1,0:T(8,128)S(1)} %fusion.42, f32[24,8,32,256]{3,2,1,0:T(8,128)} %bitcast.34), kind=kOutput, calls=%fused_computation | convolution fusion | flops 1207959552 | bytes 8437760 | tf_op jit(solution)/shard_map/dot_general | solution.py:75
  130.7 0.7 copy-done.2
  131.5 1.3 collective-permute-start.2
  132.8 4.5 %collective-permute-start = (s32[1,256]{1,0:T(1,128)S(1)}, s32[1,256]{1,0:T(1,128)S(1)}, u32[]{:S(2)}, u32[]{:S(2)}) collective-permute-start(s32[1,256]{1,0:T(1,128)S(1)} %get-tuple-element.26), channel_id=1, source_target_pairs={{0,1},{1,8},{8,9},{9,16},{16,17},{17,24},{24,25},{2,3},{3,10},{10,... | collective-permute-start | bytes 3080 | tf_op jit(solution)/shard_map/ppermute | solution.py:15
  137.3 0.1 constant_dynamic-slice_fusion
  137.4 0.6 copy.57
  138.0 0.6 collective-permute-done
  138.6 0.2 fusion.56
  138.8 10.2 %psum.23 = f32[64,64]{1,0:T(8,128)S(1)} all-reduce(f32[64,64]{1,0:T(8,128)S(1)} %fusion.56), channel_id=1, replica_groups=mesh['row'=4,'col'=4,'ch'=2] {'ch'}, use_global_device_ids=true, to_apply=%region_3.0 | all-reduce | flops 4096 | bytes 32768 | tf_op jit(solution)/shard_map/psum | solution.py:85
  149.0 13.5 %reduce-scatter.2.cloned.1.call-done = f32[64,16,256]{2,0,1:T(8,128)} async-done(((f32[64,32,256]{2,0,1:T(8,128)}), f32[64,16,256]{2,0,1:T(8,128)}) %reduce-scatter.2.cloned.1.call-update) | async-done | bytes 1048592 | tf_op jit(solution)/shard_map/reduce_scatter | solution.py:84
  162.5 1.3 copy.56
  163.8 1.1 fusion.5
  165.0 0.6 copy.54
  165.6 2.3 collective-permute-start.1
  167.9 1.3 collective-permute-start.3
  169.3 1.3 collective-permute-start.6
  170.6 3.0 %collective-permute-start.4 = (s32[18,1]{1,0:T(8,128)S(1)}, s32[18,1]{1,0:T(8,128)S(1)}, u32[]{:S(2)}, u32[]{:S(2)}) collective-permute-start(s32[18,1]{1,0:T(8,128)S(1)} %get-tuple-element.24), channel_id=1, source_target_pairs={{0,2},{2,4},{4,6},{1,3},{3,5},{5,7},{8,10},{10,12},{12,14},{9,11},... | collective-permute-start | bytes 224 | tf_op jit(solution)/shard_map/ppermute | solution.py:15
  173.6 1.8 collective-permute-done.3
  175.5 1.4 collective-permute-start.5
  176.9 1.3 collective-permute-start.7
  178.2 0.1 add_add_fusion
  178.3 3.3 %collective-permute-done.7 = f32[64,18,1]{0,2,1:T(1,128)S(1)} collective-permute-done((f32[64,18,1]{0,2,1:T(1,128)S(1)}, f32[64,18,1]{0,2,1:T(1,128)S(1)}, u32[]{:S(2)}, u32[]{:S(2)}) %collective-permute-start.7) | collective-permute-done | bytes 4640 | tf_op jit(solution)/shard_map/ppermute | solution.py:18
  181.6 4.8 %fusion.27 = f32[64,16,256]{0,2,1:T(8,128)S(1)} fusion(f32[64,18,1]{0,2,1:T(1,128)S(1)} %collective-permute-done.7, f32[64,1,256]{0,2,1:T(8,128)S(1)} %collective-permute-done.3, f32[64,16,256]{0,2,1:T(8,128)S(1)} %bitcast.37, f32[64,1,256]{0,2,1:T(8,128)S(1)} %collective-permute-done.1, f32[64,18,1]{0,2,1:T(1,128)S(1)} %collective-permute-done.5, ...), kind=kLoop, calls=%fused_computation.46 | loop fusion | flops 4456448 | bytes 2319360 | tf_op jit(solution)/shard_map/div | solution.py:38
  186.4 4.7 %collective-permute-start.8 = (f32[64,1,256]{0,2,1:T(8,128)S(1)}, f32[64,1,256]{0,2,1:T(8,128)S(1)}, u32[]{:S(2)}, u32[]{:S(2)}) collective-permute-start(f32[64,1,256]{0,2,1:T(8,128)S(1)} %get-tuple-element.19), channel_id=1, source_target_pairs={{0,1},{1,8},{8,9},{9,16},{16,17},{17,24},{24,25},{2,3},{3,10},{10,... | collective-permute-start | bytes 196616 | tf_op jit(solution)/shard_map/ppermute | solution.py:15
  191.1 1.3 collective-permute-start.9
  192.4 1.2 collective-permute-done.8
  193.6 4.6 %collective-permute-done.9 = f32[64,1,256]{0,2,1:T(8,128)S(1)} collective-permute-done((f32[64,1,256]{0,2,1:T(8,128)S(1)}, f32[64,1,256]{0,2,1:T(8,128)S(1)}, u32[]{:S(2)}, u32[]{:S(2)}) %collective-permute-start.9) | collective-permute-done | bytes 65568 | tf_op jit(solution)/shard_map/ppermute | solution.py:18
  198.3 2.9 %collective-permute-start.10 = (f32[64,18,1]{0,2,1:T(1,128)S(1)}, f32[64,18,1]{0,2,1:T(1,128)S(1)}, u32[]{:S(2)}, u32[]{:S(2)}) collective-permute-start(f32[64,18,1]{0,2,1:T(1,128)S(1)} %get-tuple-element.13), channel_id=1, source_target_pairs={{0,2},{2,4},{4,6},{1,3},{3,5},{5,7},{8,10},{10,12},{12,14},{9,11},... | collective-permute-start | bytes 13832 | tf_op jit(solution)/shard_map/ppermute | solution.py:15
  201.2 1.3 collective-permute-start.11
  202.5 2.5 collective-permute-done.11
  204.9 4.8 %fusion.18 = f32[64,16,256]{0,2,1:T(8,128)S(1)} fusion(f32[64,18,1]{0,2,1:T(1,128)S(1)} %collective-permute-done.11, f32[64,1,256]{0,2,1:T(8,128)S(1)} %collective-permute-done.9, f32[64,16,256]{0,2,1:T(8,128)S(1)} %fusion.27, f32[64,1,256]{0,2,1:T(8,128)S(1)} %collective-permute-done.8, f32[64,18,1]{0,2,1:T(1,128)S(1)} %collective-permute-done.10, ...), kind=kLoop, calls=%fused_computation.29 | loop fusion | flops 4456448 | bytes 2319360 | tf_op jit(solution)/shard_map/div | solution.py:38
  209.8 4.3 %collective-permute-start.12 = (f32[64,1,256]{0,2,1:T(8,128)S(1)}, f32[64,1,256]{0,2,1:T(8,128)S(1)}, u32[]{:S(2)}, u32[]{:S(2)}) collective-permute-start(f32[64,1,256]{0,2,1:T(8,128)S(1)} %get-tuple-element.17), channel_id=1, source_target_pairs={{0,1},{1,8},{8,9},{9,16},{16,17},{17,24},{24,25},{2,3},{3,10},{10,... | collective-permute-start | bytes 196616 | tf_op jit(solution)/shard_map/ppermute | solution.py:15
  214.1 1.3 collective-permute-start.13
  215.4 1.2 collective-permute-done.12
  216.6 4.6 %collective-permute-done.13 = f32[64,1,256]{0,2,1:T(8,128)S(1)} collective-permute-done((f32[64,1,256]{0,2,1:T(8,128)S(1)}, f32[64,1,256]{0,2,1:T(8,128)S(1)}, u32[]{:S(2)}, u32[]{:S(2)}) %collective-permute-start.13) | collective-permute-done | bytes 65568 | tf_op jit(solution)/shard_map/ppermute | solution.py:18
  221.3 2.9 %collective-permute-start.14 = (f32[64,18,1]{0,2,1:T(1,128)S(1)}, f32[64,18,1]{0,2,1:T(1,128)S(1)}, u32[]{:S(2)}, u32[]{:S(2)}) collective-permute-start(f32[64,18,1]{0,2,1:T(1,128)S(1)} %get-tuple-element.11), channel_id=1, source_target_pairs={{0,2},{2,4},{4,6},{1,3},{3,5},{5,7},{8,10},{10,12},{12,14},{9,11},... | collective-permute-start | bytes 13832 | tf_op jit(solution)/shard_map/ppermute | solution.py:15
  224.2 1.3 collective-permute-start.15
  225.5 2.5 collective-permute-done.15
  228.0 4.8 %fusion.9 = f32[1,64,16,256]{1,3,2,0:T(8,128)S(1)} fusion(f32[64,18,1]{0,2,1:T(1,128)S(1)} %collective-permute-done.15, f32[64,1,256]{0,2,1:T(8,128)S(1)} %collective-permute-done.13, f32[64,16,256]{0,2,1:T(8,128)S(1)} %fusion.18, f32[64,1,256]{0,2,1:T(8,128)S(1)} %collective-permute-done.12, f32[64,18,1]{0,2,1:T(1,128)S(1)} %collective-permute-done.14, ...), kind=kLoop, calls=%fused_computation.12 | loop fusion | flops 4456448 | bytes 2319360 | tf_op jit(solution)/shard_map/stack | solution.py:95
  232.8 2.4 pad_maximum_fusion
  235.2 3.4 %copy.52 = f32[2,64,16,256]{3,2,1,0:T(8,128)S(1)} copy(f32[2,64,16,256]{1,3,2,0:T(8,128)} %pad_maximum_fusion) | data formatting | bytes 4194304 | tf_op jit(solution)/shard_map/stack | solution.py:95
  238.6 27.3 %all_to_all.5 = f32[2,64,16,256]{3,2,1,0:T(8,128)S(1)} all-to-all(f32[2,64,16,256]{3,2,1,0:T(8,128)S(1)} %copy.52), channel_id=1, replica_groups=mesh['row'=4,'col'=4,'ch'=2] {'ch'}, dimensions={0} | all-to-all | bytes 4194304 | tf_op jit(solution)/shard_map/all_to_all | solution.py:96
  265.9 1.5 copy.53
  (27 shorter events, 0.3 us)
Async XLA Ops:
  7.2 7.1 %copy-start = (f32[64,32,256]{2,1,0:T(8,128)S(1)}, f32[64,32,256]{2,1,0:T(8,128)}, u32[]{:S(2)}) copy-start(f32[64,32,256]{2,1,0:T(8,128)} %param.5) | copy-start | bytes 6291460
  7.2 111.1 %all-reduce.3.cloned.1.call-start = ((), (), s32[]{:S(2)}) async-start(), calls=%async_computation.3 | async-start | bytes 196608 | tf_op jit(solution)/shard_map/psum | solution.py:64
  14.2 104.0 %copy-start.3 = (f32[64,192]{1,0:T(8,128)S(1)}, f32[64,192]{1,0:T(8,128)}, u32[]{:S(2)}) copy-start(f32[64,192]{1,0:T(8,128)} %param.6) | copy-start | bytes 147460
  26.5 136.1 %reduce-scatter.2.cloned.1.call-start = ((), (), s32[]{:S(2)}) async-start(), calls=%async_computation.2 | async-start | bytes 3145728 | tf_op jit(solution)/shard_map/reduce_scatter | solution.py:84
  119.3 19.3 %copy-start.1 = (f32[64,192]{1,0:T(8,128)}, f32[64,192]{1,0:T(8,128)S(1)}, u32[]{:S(2)}) copy-start(f32[64,192]{1,0:T(8,128)S(1)} %fusion.42) | copy-start | bytes 147460
  130.7 0.8 copy-start.2
  131.5 6.6 %collective-permute-start.2 = (s32[1,256]{1,0:T(1,128)S(1)}, s32[1,256]{1,0:T(1,128)S(1)}, u32[]{:S(2)}, u32[]{:S(2)}) collective-permute-start(s32[1,256]{1,0:T(1,128)S(1)} %get-tuple-element.25), channel_id=1, source_target_pairs={{1,0},{8,1},{9,8},{16,9},{17,16},{24,17},{25,24},{3,2},{10,3},{11,... | collective-permute-start | bytes 3080 | tf_op jit(solution)/shard_map/ppermute | solution.py:18
  132.8 5.8 %collective-permute-start = (s32[1,256]{1,0:T(1,128)S(1)}, s32[1,256]{1,0:T(1,128)S(1)}, u32[]{:S(2)}, u32[]{:S(2)}) collective-permute-start(s32[1,256]{1,0:T(1,128)S(1)} %get-tuple-element.26), channel_id=1, source_target_pairs={{0,1},{1,8},{8,9},{9,16},{16,17},{17,24},{24,25},{2,3},{3,10},{10,... | collective-permute-start | bytes 3080 | tf_op jit(solution)/shard_map/ppermute | solution.py:15
  165.6 8.0 %collective-permute-start.1 = (f32[64,1,256]{0,2,1:T(8,128)S(1)}, f32[64,1,256]{0,2,1:T(8,128)S(1)}, u32[]{:S(2)}, u32[]{:S(2)}) collective-permute-start(f32[64,1,256]{0,2,1:T(8,128)S(1)} %get-tuple-element.21), channel_id=1, source_target_pairs={{0,1},{1,8},{8,9},{9,16},{16,17},{17,24},{24,25},{2,3},{3,10},{10,... | collective-permute-start | bytes 196616 | tf_op jit(solution)/shard_map/ppermute | solution.py:15
  167.9 7.6 %collective-permute-start.3 = (f32[64,1,256]{0,2,1:T(8,128)S(1)}, f32[64,1,256]{0,2,1:T(8,128)S(1)}, u32[]{:S(2)}, u32[]{:S(2)}) collective-permute-start(f32[64,1,256]{0,2,1:T(8,128)S(1)} %get-tuple-element.22), channel_id=1, source_target_pairs={{1,0},{8,1},{9,8},{16,9},{17,16},{24,17},{25,24},{3,2},{10,3},{11,... | collective-permute-start | bytes 196616 | tf_op jit(solution)/shard_map/ppermute | solution.py:18
  169.3 8.9 %collective-permute-start.6 = (s32[18,1]{1,0:T(8,128)S(1)}, s32[18,1]{1,0:T(8,128)S(1)}, u32[]{:S(2)}, u32[]{:S(2)}) collective-permute-start(s32[18,1]{1,0:T(8,128)S(1)} %get-tuple-element.23), channel_id=1, source_target_pairs={{2,0},{4,2},{6,4},{3,1},{5,3},{7,5},{10,8},{12,10},{14,12},{11,9},... | collective-permute-start | bytes 224 | tf_op jit(solution)/shard_map/ppermute | solution.py:18
  170.6 7.6 %collective-permute-start.4 = (s32[18,1]{1,0:T(8,128)S(1)}, s32[18,1]{1,0:T(8,128)S(1)}, u32[]{:S(2)}, u32[]{:S(2)}) collective-permute-start(s32[18,1]{1,0:T(8,128)S(1)} %get-tuple-element.24), channel_id=1, source_target_pairs={{0,2},{2,4},{4,6},{1,3},{3,5},{5,7},{8,10},{10,12},{12,14},{9,11},... | collective-permute-start | bytes 224 | tf_op jit(solution)/shard_map/ppermute | solution.py:15
  175.5 2.8 %collective-permute-start.5 = (f32[64,18,1]{0,2,1:T(1,128)S(1)}, f32[64,18,1]{0,2,1:T(1,128)S(1)}, u32[]{:S(2)}, u32[]{:S(2)}) collective-permute-start(f32[64,18,1]{0,2,1:T(1,128)S(1)} %get-tuple-element.15), channel_id=1, source_target_pairs={{0,2},{2,4},{4,6},{1,3},{3,5},{5,7},{8,10},{10,12},{12,14},{9,11},... | collective-permute-start | bytes 13832 | tf_op jit(solution)/shard_map/ppermute | solution.py:15
  176.9 4.7 %collective-permute-start.7 = (f32[64,18,1]{0,2,1:T(1,128)S(1)}, f32[64,18,1]{0,2,1:T(1,128)S(1)}, u32[]{:S(2)}, u32[]{:S(2)}) collective-permute-start(f32[64,18,1]{0,2,1:T(1,128)S(1)} %get-tuple-element.16), channel_id=1, source_target_pairs={{2,0},{4,2},{6,4},{3,1},{5,3},{7,5},{10,8},{12,10},{14,12},{11,9},... | collective-permute-start | bytes 13832 | tf_op jit(solution)/shard_map/ppermute | solution.py:18
  186.4 7.2 %collective-permute-start.8 = (f32[64,1,256]{0,2,1:T(8,128)S(1)}, f32[64,1,256]{0,2,1:T(8,128)S(1)}, u32[]{:S(2)}, u32[]{:S(2)}) collective-permute-start(f32[64,1,256]{0,2,1:T(8,128)S(1)} %get-tuple-element.19), channel_id=1, source_target_pairs={{0,1},{1,8},{8,9},{9,16},{16,17},{17,24},{24,25},{2,3},{3,10},{10,... | collective-permute-start | bytes 196616 | tf_op jit(solution)/shard_map/ppermute | solution.py:15
  191.1 7.1 %collective-permute-start.9 = (f32[64,1,256]{0,2,1:T(8,128)S(1)}, f32[64,1,256]{0,2,1:T(8,128)S(1)}, u32[]{:S(2)}, u32[]{:S(2)}) collective-permute-start(f32[64,1,256]{0,2,1:T(8,128)S(1)} %get-tuple-element.20), channel_id=1, source_target_pairs={{1,0},{8,1},{9,8},{16,9},{17,16},{24,17},{25,24},{3,2},{10,3},{11,... | collective-permute-start | bytes 196616 | tf_op jit(solution)/shard_map/ppermute | solution.py:18
  198.3 4.2 %collective-permute-start.10 = (f32[64,18,1]{0,2,1:T(1,128)S(1)}, f32[64,18,1]{0,2,1:T(1,128)S(1)}, u32[]{:S(2)}, u32[]{:S(2)}) collective-permute-start(f32[64,18,1]{0,2,1:T(1,128)S(1)} %get-tuple-element.13), channel_id=1, source_target_pairs={{0,2},{2,4},{4,6},{1,3},{3,5},{5,7},{8,10},{10,12},{12,14},{9,11},... | collective-permute-start | bytes 13832 | tf_op jit(solution)/shard_map/ppermute | solution.py:15
  201.2 3.8 %collective-permute-start.11 = (f32[64,18,1]{0,2,1:T(1,128)S(1)}, f32[64,18,1]{0,2,1:T(1,128)S(1)}, u32[]{:S(2)}, u32[]{:S(2)}) collective-permute-start(f32[64,18,1]{0,2,1:T(1,128)S(1)} %get-tuple-element.14), channel_id=1, source_target_pairs={{2,0},{4,2},{6,4},{3,1},{5,3},{7,5},{10,8},{12,10},{14,12},{11,9},... | collective-permute-start | bytes 13832 | tf_op jit(solution)/shard_map/ppermute | solution.py:18
  209.8 6.8 %collective-permute-start.12 = (f32[64,1,256]{0,2,1:T(8,128)S(1)}, f32[64,1,256]{0,2,1:T(8,128)S(1)}, u32[]{:S(2)}, u32[]{:S(2)}) collective-permute-start(f32[64,1,256]{0,2,1:T(8,128)S(1)} %get-tuple-element.17), channel_id=1, source_target_pairs={{0,1},{1,8},{8,9},{9,16},{16,17},{17,24},{24,25},{2,3},{3,10},{10,... | collective-permute-start | bytes 196616 | tf_op jit(solution)/shard_map/ppermute | solution.py:15
  214.1 7.1 %collective-permute-start.13 = (f32[64,1,256]{0,2,1:T(8,128)S(1)}, f32[64,1,256]{0,2,1:T(8,128)S(1)}, u32[]{:S(2)}, u32[]{:S(2)}) collective-permute-start(f32[64,1,256]{0,2,1:T(8,128)S(1)} %get-tuple-element.18), channel_id=1, source_target_pairs={{1,0},{8,1},{9,8},{16,9},{17,16},{24,17},{25,24},{3,2},{10,3},{11,... | collective-permute-start | bytes 196616 | tf_op jit(solution)/shard_map/ppermute | solution.py:18
  221.3 4.2 %collective-permute-start.14 = (f32[64,18,1]{0,2,1:T(1,128)S(1)}, f32[64,18,1]{0,2,1:T(1,128)S(1)}, u32[]{:S(2)}, u32[]{:S(2)}) collective-permute-start(f32[64,18,1]{0,2,1:T(1,128)S(1)} %get-tuple-element.11), channel_id=1, source_target_pairs={{0,2},{2,4},{4,6},{1,3},{3,5},{5,7},{8,10},{10,12},{12,14},{9,11},... | collective-permute-start | bytes 13832 | tf_op jit(solution)/shard_map/ppermute | solution.py:15
  224.2 3.8 %collective-permute-start.15 = (f32[64,18,1]{0,2,1:T(1,128)S(1)}, f32[64,18,1]{0,2,1:T(1,128)S(1)}, u32[]{:S(2)}, u32[]{:S(2)}) collective-permute-start(f32[64,18,1]{0,2,1:T(1,128)S(1)} %get-tuple-element.12), channel_id=1, source_target_pairs={{2,0},{4,2},{6,4},{3,1},{5,3},{7,5},{10,8},{12,10},{14,12},{11,9},... | collective-permute-start | bytes 13832 | tf_op jit(solution)/shard_map/ppermute | solution.py:18
Sparse Core Ops, SparseCore 0:
  26.6 91.6 all-reduce.2
  130.8 31.6 reduce-scatter.1
